TPU v7x, 512 devices: a whole 4x4x16 slice. The times are simulated.
512 devices in a mesh: pool: 64 (over z, y), head: 8 (over x, core).
Axes of the slice: x: 4, y: 4, z: 16, core: 2. Of those that a mesh axis runs over, the one named last changes fastest.
Arguments:
- kv_store: bfloat16 [128, 2, 64, 1024], P('pool', None, None, 'head'), may hold values from -6 to 6
- fresh_q: bfloat16 [64, 24, 8192], P('pool', None, 'head'), may hold values from -160 to 160
- fresh_kv: bfloat16 [64, 24, 2, 1024], P('pool', None, None, 'head'), may hold values from -6 to 6
- dec_q: bfloat16 [32, 8192], P(None, 'head'), may hold values from -160 to 160
- dec_kv: bfloat16 [32, 2, 1024], P(None, None, 'head'), may hold values from -6 to 6
- out_weight: bfloat16 [8192, 8192], P('head', 'pool'), may hold values from -0.0625 to 0.0625
- span_slot: int32 [64], replicated, may hold values from 0 to 127, as said below
- span_order: int32 [64], replicated, may hold values from 0 to 63, each once
- span_start: int32 [64], replicated, may hold values from 0 to 4536, as said below
- pick: int32 [64, 24], replicated, may hold values from 0 to 63, as said below
- dec_len: int32 [32], replicated, may hold values from 1 to 64, as said below
Outputs:
- fresh_out: bfloat16 [64, 24, 8192], P('pool', None, 'head')
- dec_proj: bfloat16 [32, 8192], P(None, 'pool')
Inputs may be any that keep to these rules, and one draw needn't show every extreme that they name: `span_slot`: distinct values. Storage rows k * 2 to (k + 1) * 2 - 1 belong to pool device k; some device holds 2 spans in every draw. span_start[0] = 0 and span_start[s + 1] - span_start[s] lies between 64 and 80. `pick`: each row holds 24 distinct indices in increasing order. `dec_len`: some row reads all 64 slots in every draw.
All inputs are finite; a program needn't handle non-finite values.
Results may differ from a plain program's by a relative error of at most 0.018.
Values may be sent and summed in bfloat16 or wider, within the bound.
A program may use at most 64 MiB of HBM per device.

v0:
```python
import jax
import jax.numpy as jnp
from jax import lax
from jax.sharding import PartitionSpec as P

QH = 64
KVH = 8
HD = 128
L = 64
R = 24


NEG = -1e30
BASE = 500000.0


def merged_2(value, axis, combine):
    everything = jax.tree.map(
        lambda part, kind: lax.all_gather(part.astype(kind), axis),
        value,
        jax.tree.map(lambda a: jnp.bfloat16 if a.dtype == jnp.float32 else a.dtype, value),
    )

    def take(k):
        return jax.tree.map(lambda part, own: part[k].astype(own.dtype), everything, value)

    return lax.fori_loop(
        1, lax.axis_size(axis), lambda k, so_far: combine(so_far, take(k)), take(0)
    )


def frequencies(half):
    return jnp.power(BASE, -jnp.arange(half, dtype=jnp.float32) / half)


def rotate(heads, positions):
    half = heads.shape[-1] // 2
    angle = positions.astype(jnp.float32)[:, None, None] * frequencies(half)
    cosine = jnp.cos(angle)
    sine = jnp.sin(angle)
    first = heads[..., :half]
    second = heads[..., half:]
    return jnp.concatenate(
        [first * cosine - second * sine, second * cosine + first * sine], axis=-1
    )


def to_groups(rows_in, group):
    count = rows_in.shape[0]
    shaped = rows_in.reshape(count, -1, group, HD)
    local = shaped.shape[1]
    return shaped.transpose(1, 0, 2, 3).reshape(local, count * group, HD)


def from_groups(merged, count, group):
    local = merged.shape[0]
    return (
        merged.reshape(local, count, group, HD)
        .transpose(1, 0, 2, 3)
        .reshape(count, local * group * HD)
    )


def by_head(rows_in):
    count = rows_in.shape[0]
    return rows_in.reshape(count, -1, HD).transpose(1, 0, 2)


def empty_state(local, count):
    return (
        jnp.full((local, count), NEG, jnp.float32),
        jnp.zeros((local, count), jnp.float32),
        jnp.zeros((local, count, HD), jnp.float32),
    )


def absorb(state, queries, key_block, value_block, visible):
    highest, total, accum = state
    scale = HD ** (-0.5)
    scores = (
        jnp.einsum("gqd,gkd->gqk", queries, key_block, preferred_element_type=jnp.float32) * scale
    )
    scores = jnp.where(visible[None], scores, NEG)
    raised = jnp.maximum(highest, jnp.max(scores, axis=-1))
    weights = jnp.where(visible[None], jnp.exp(scores - raised[..., None]), 0.0)
    factor = jnp.exp(highest - raised)
    total = total * factor + jnp.sum(weights, axis=-1)
    accum = accum * factor[..., None] + jnp.einsum(
        "gqk,gkd->gqd",
        weights.astype(jnp.bfloat16),
        value_block,
        preferred_element_type=jnp.float32,
    )
    return (raised, total, accum)


def combine(first, second):
    raised = jnp.maximum(first[0], second[0])
    left = jnp.exp(first[0] - raised)
    right = jnp.exp(second[0] - raised)
    return (
        raised,
        first[1] * left + second[1] * right,
        first[2] * left[..., None] + second[2] * right[..., None],
    )


def shards(
    kv_store,
    fresh_q,
    fresh_kv,
    dec_q,
    dec_kv,
    out_weight,
    span_slot,
    span_order,
    span_start,
    pick,
    dec_len,
):
    group = QH // KVH
    my_slot = lax.axis_index("pool")
    slots = span_order.shape[0]
    stored = kv_store.shape[0]
    store_total = stored * lax.axis_size("pool")
    local = fresh_kv.shape[-1] // HD
    rows = dec_q.shape[0]
    span_ids = jnp.arange(slots, dtype=jnp.int32)
    span_place = jnp.sum(
        jnp.where(span_order[None, :] == span_ids[:, None], span_ids[None, :], 0), axis=1
    )
    store_ids = jnp.arange(store_total, dtype=jnp.int32)
    holding = span_slot[None, :] == store_ids[:, None]
    store_live = jnp.any(holding, axis=1)
    store_place = jnp.sum(jnp.where(holding, span_place[None, :], 0), axis=1)
    columns = jnp.arange(L, dtype=jnp.int32)
    picked = jnp.any(pick[:, :, None] == columns[None, None, :], axis=1)
    own_pick = lax.dynamic_index_in_dim(pick, my_slot, 0, keepdims=False)
    own_start = lax.dynamic_index_in_dim(span_start, my_slot, 0, keepdims=False)
    query_place = own_start + own_pick
    rotated_q = rotate(fresh_q[0].reshape(R, -1, HD).astype(jnp.float32), query_place).astype(
        jnp.bfloat16
    )
    queries = to_groups(rotated_q.reshape(R, -1), group)
    query_reach = jnp.repeat(query_place, group)
    every_fresh = lax.all_gather(fresh_kv, "pool", axis=0, tiled=True)
    fresh_place = (span_start[:, None] + pick).reshape(-1)
    turned_fresh = rotate(
        every_fresh[:, :, 0].reshape(slots * R, -1, HD).astype(jnp.float32), fresh_place
    ).astype(jnp.bfloat16)
    fresh_keys = by_head(turned_fresh.reshape(slots * R, -1))
    fresh_values = by_head(every_fresh[:, :, 1].reshape(slots * R, -1))
    recompute_state = absorb(
        empty_state(local, R * group),
        queries,
        fresh_keys,
        fresh_values,
        fresh_place[None, :] <= query_reach[:, None],
    )
    dec_queries = to_groups(dec_q, group)
    row_len = jnp.repeat(dec_len, group)

    def view(item, place):
        turned = rotate(
            item[0].reshape(L, -1, HD).astype(jnp.float32), jnp.full((L,), span_start[place])
        ).astype(jnp.bfloat16)
        reach = span_start[place] + columns
        keep = jnp.logical_not(lax.dynamic_index_in_dim(picked, place, 0, keepdims=False))
        return (by_head(turned.reshape(L, -1)), by_head(item[1]), reach, keep)

    initial = (recompute_state,)

    def wanted(place):
        return place <= my_slot

    def block_step(carry, key_block, value_block, reach, keep):
        seen = keep[None, :] & (reach[None, :] <= query_reach[:, None])
        return (absorb(carry[0], queries, key_block, value_block, seen),)

    piece = lax.all_gather(kv_store, "pool", axis=0, tiled=True)

    def one_row(inner, inputs):
        item, index = inputs
        place = store_place[index]

        def apply(state_in):
            key_block, value_block, reach, keep = view(item, place)
            return block_step(state_in, key_block, value_block, reach, keep)

        return (
            lax.cond(store_live[index] & wanted(place), apply, lambda state_in: state_in, inner),
            None,
        )

    indices = jnp.arange(piece.shape[0], dtype=jnp.int32)
    result, _ = lax.scan(one_row, initial, (piece, indices))
    own_keys = lax.dynamic_slice_in_dim(fresh_keys, my_slot * R, R, 1)
    own_values = lax.dynamic_slice_in_dim(fresh_values, my_slot * R, R, 1)
    seen_fresh = jnp.broadcast_to((my_slot < row_len)[:, None], (rows * group, R))
    dec_state = absorb(
        empty_state(local, rows * group), dec_queries, own_keys, own_values, seen_fresh
    )

    def make_apply(item, place):

        def apply(state_in):
            key_block, value_block, reach, keep = view(item, place)
            return absorb(
                state_in,
                dec_queries,
                key_block,
                value_block,
                keep[None, :] & (place < row_len)[:, None],
            )

        return apply

    for offset in range(stored):
        index = my_slot * stored + offset
        place = store_place[index]
        dec_state = lax.cond(
            store_live[index],
            make_apply(kv_store[offset], place),
            lambda state_in: state_in,
            dec_state,
        )
    dec_state = merged_2(dec_state, "pool", combine)
    recompute_final = result[0]
    attended = recompute_final[2] / recompute_final[1][..., None]
    fresh_out = from_groups(attended, R, group).astype(jnp.bfloat16)[None]
    token_keys = by_head(dec_kv[:, 0])
    token_values = by_head(dec_kv[:, 1])
    token_seen = (jnp.arange(rows * group, dtype=jnp.int32) // group)[:, None] == jnp.arange(
        rows, dtype=jnp.int32
    )[None, :]
    dec_state = absorb(dec_state, dec_queries, token_keys, token_values, token_seen)
    dec_attn = from_groups(dec_state[2] / dec_state[1][..., None], rows, group).astype(jnp.bfloat16)
    partial_terms = jnp.dot(dec_attn, out_weight, preferred_element_type=jnp.float32)
    dec_proj = lax.psum(partial_terms, "head").astype(jnp.bfloat16)
    return (fresh_out, dec_proj)


def solution(mesh):
    return jax.shard_map(
        shards,
        mesh=mesh,
        in_specs=(
            P("pool", None, None, "head"),
            P("pool", None, "head"),
            P("pool", None, None, "head"),
            P(None, "head"),
            P(None, None, "head"),
            P("head", "pool"),
            P(),
            P(),
            P(),
            P(),
            P(),
        ),
        out_specs=(P("pool", None, "head"), P(None, "pool")),
        check_vma=False,
    )
```

profile of v0, /device:TPU:504, one launch (start us, length us, event | category | flops | bytes accessed | tf_op | source)
XLA Modules:
  0.0 1444.8 jit_solution(17761273239110863424)
XLA Ops:
  17.9 92.9 %all_gather.24 = bf16[64,24,2,128]{3,1,0,2:T(8,128)(2,1)S(1)} all-gather(bf16[1,24,2,128]{3,1,0,2:T(8,128)(2,1)S(1)} %copy.26), channel_id=1, replica_groups=mesh['pool'=64,'head'=8] {'pool'}, dimensions={0}, use_global_device_ids=true | all-gather | bytes 798720 | tf_op jit(solution)/shard_map/all_gather | solution.py:146
  123.2 84.2 %all-gather.3 = bf16[64,1,256]{2,1,0:T(2,128)(2,1)S(1)} all-gather(bf16[1,1,256]{2,1,0:T(2,128)(2,1)S(1)} %convert_bitcast_fusion.2), channel_id=2, replica_groups=mesh['pool'=64,'head'=8] {'pool'}, dimensions={0}, use_global_device_ids=true | all-gather | bytes 33280 | tf_op jit(solution)/shard_map/all_gather | solution.py:19
  207.4 80.0 %all-gather.4 = bf16[64,1,256]{2,1,0:T(2,128)(2,1)S(1)} all-gather(bf16[1,1,256]{2,1,0:T(2,128)(2,1)S(1)} %convert_bitcast_fusion.1), channel_id=3, replica_groups=mesh['pool'=64,'head'=8] {'pool'}, dimensions={0}, use_global_device_ids=true | all-gather | bytes 33280 | tf_op jit(solution)/shard_map/all_gather | solution.py:19
  289.7 1055.2 %while.35 = (s32[]{:T(128)}, f32[1,192]{1,0:T(1,128)S(1)}, f32[1,192]{1,0:T(1,128)S(1)}, f32[1,192,128]{2,1,0:T(8,128)S(1)}, s32[128]{0:T(128)S(1)}, /*index=5*/...) while((s32[]{:T(128)}, f32[1,192]{1,0:T(1,128)S(1)}, ...), condition=%wide.region_11.12_spmd.clone, body=%wide.region_6.11_spmd.clone.sunk | while | flops 6599373 | bytes 545140 | solution.py:196
  294.7 6.3 conditional.7
  316.3 6.3 conditional.7
  332.8 6.3 conditional.7
  359.4 6.3 conditional.7
  370.8 6.3 conditional.7
  382.2 6.3 conditional.7
  393.7 6.3 conditional.7
  405.1 6.3 conditional.7
  416.5 6.3 conditional.7
  427.9 6.3 conditional.7
  487.5 6.3 conditional.7
  498.9 6.3 conditional.7
  510.3 6.3 conditional.7
  531.9 6.3 conditional.7
  604.2 6.3 conditional.7
  1087.4 6.3 conditional.7
  1153.4 6.3 conditional.7
  1242.2 6.3 conditional.7
  1346.5 66.8 %while.34 = (s32[]{:T(128)}, f32[1,256]{1,0:T(1,128)S(1)}, f32[1,256]{1,0:T(1,128)S(1)}, f32[1,256,128]{2,1,0:T(8,128)S(1)}, bf16[64,1,256]{2,1,0:T(2,128)(2,1)S...) while((s32[]{:T(128)}, f32[1,256]{1,0:T(1,128)S(1)}, ...), condition=%wide.region_23.24_spmd, body=%wide.region_22.23_spmd.sunk | while | flops 133125 | bytes 337047 | solution.py:27
  1413.8 24.1 %psum.7 = bf16[32,128]{1,0:T(8,128)(2,1)} all-reduce(f32[32,128]{1,0:T(8,128)S(1)} %fusion.141), channel_id=1, replica_groups=mesh['pool'=64,'head'=8] {'head'}, use_global_device_ids=true, to_apply=%region_26.27 | all-reduce | flops 4096 | bytes 24576 | tf_op jit(solution)/shard_map/psum | solution.py:239
  (1737 shorter events, 867.4 us)
Async XLA Ops:
  7.2 1406.5 %copy-start = (bf16[1024,128]{1,0:T(8,128)(2,1)S(1)}, bf16[1024,128]{1,0:T(8,128)(2,1)}, u32[]{:S(2)}) copy-start(bf16[1024,128]{1,0:T(8,128)(2,1)} %param.26) | copy-start | bytes 786436
  7.2 282.5 %all-gather.8.cloned.1.call-start = ((), (), s32[]{:S(2)}) async-start(), calls=%async_computation | async-start | bytes 4259840 | tf_op jit(solution)/shard_map/all_gather | solution.py:180
  7.9 1337.7 %all-gather.10.cloned.1.call-start = ((), (), s32[]{:S(2)}) async-start(), calls=%async_computation.1 | async-start | bytes 4259840 | tf_op jit(solution)/shard_map/all_gather | solution.py:19
  110.9 4.5 copy-start.1
  114.6 0.9 copy-start.5
  114.8 6.6 copy-start.4
  115.1 7.0 copy-start.2
  288.7 0.7 copy-start.3
Sparse Core Ops, SparseCore 0:
  10.9 140.9 all-gather.7
  154.8 141.1 all-gather.9
where the time goes:
time: 1470 us; the launch traced here: 1440 us
  loops' own time  579 us (39%)
  local copies, waits for them, and re-layouts  303 us (21%)
  blocking collectives  281 us (19%)
  other arithmetic  184 us (13%)
  matrix products  81.1 us (6%)
  between operations  15.7 us (1%)
    another operation x1, loops' own time, shards(): result, _ = lax.scan(one_row, initial, (piece, indices))  406 us
    another operation x128, loops' own time, one_row(): lax.cond(store_live[index] & wanted(place), apply, lambda state_in: state...  169 us
    all_gather x2, blocking collectives, merged_2(): lax.all_gather(part.astype(kind), axis)  164 us
    all_gather x1, blocking collectives, shards(): every_fresh = lax.all_gather(fresh_kv, 'pool', axis=0, tiled=True)  92.9 us
    dynamic_slice x128, local copies, waits for them, and re-layouts, shards(): result, _ = lax.scan(one_row, initial, (piece, indices))  82.3 us
    dynamic_slice x128, local copies, waits for them, and re-layouts, one_row(): place = store_place[index]  81.7 us
    dynamic_slice x128, local copies, waits for them, and re-layouts, one_row(): store_live[index] & wanted(place)  78.2 us
    dot_general x68, matrix products, absorb(): jnp.einsum('gqk,gkd->gqd', weights.astype(jnp.bfloat16), value_block, pre...  66.1 us
  transfers between devices with their start and end apart: 2, of which 0 were waited for; matrix products, arithmetic and copies ran while one was open for 35% of the time, Pallas kernels for 0%

commit v1 on v0

v1 whole, which is shorter than its diff:
```python
import functools
import math

import jax
import jax.numpy as jnp
import numpy as np
from jax import lax
from jax.experimental import pallas as pl
from jax.experimental.pallas import tpu as pltpu
from jax.sharding import PartitionSpec as P

QH, KVH, HD = 64, 8, 128
G = QH // KVH
L, R, SLOTS, ROWS = 64, 24, 64, 32
NZ, NY, NX, NH = 16, 4, 4, 8
BASE = 500000.0
NEG = -1e30
FLOOR = -1e20
BIG = 1e9
C2 = HD**-0.5 * math.log2(math.e)
CH = 304
PIECES = ((0, 128), (128, 176))
NP = len(PIECES)
OWN, FAR = 14, 15
QB = 256
NQB = 1024 // QB
MESH = pl.DeviceIdType.MESH
F32 = jnp.float32
BF16 = jnp.bfloat16


def nt(a, b):
    return lax.dot_general(a, b, (((1,), (1,)), ((), ())), preferred_element_type=F32)


def tn(a, b):
    return lax.dot_general(a, b, (((0,), (0,)), ((), ())), preferred_element_type=F32)


def iota(shape, dim):
    return lax.broadcasted_iota(jnp.int32, shape, dim)


def turn(x, cosine, sine):
    return x * cosine + pltpu.roll(x, HD // 2, 1) * sine


def kernel(
    kv, fq, fkv, dq, dkv, w, slot, order, start, pick, dlen, freq,
    fresh_out, dec_out,
    kin, fqv, fkvv, dqv, dkvv, wv, slotv, orderv, startv, pickv, dlenv, freqv,
    chunks, queries, places, bounds, top, tot, acc,
    dsend, dstat, fsend, fstat, drecv, dsrecv, frecv, fsrecv, halfs, terms,
    in_sem, rs_sem, rr_sem, ls_sem, lr_sem, qs_sem, qr_sem,
    ds_sem, dr_sem, fs_sem, fr_sem, xs_sem, xr_sem,
):
    me = lax.axis_index("pool")
    head = lax.axis_index("head")
    z = me // NY
    y = me % NY
    ring = NZ * NY
    zpeer = {(n, way): (me + ring + (n if way == 0 else -n) * NY) % ring for n in (1, 2) for way in (0, 1)}
    ypeer = [z * NY + (y + d) % NY for d in range(NY)]
    core = head % 2
    column = head // 2
    mate = head + 1 - 2 * core
    xpeer = [(head + 2 * e) % NH for e in range(NX)]

    barrier = pltpu.get_barrier_semaphore()
    targets = [(zpeer[n, way], head) for n in (1, 2) for way in (0, 1)]
    targets += [(ypeer[d], head) for d in range(1, NY)]
    targets += [(me, mate)] + [(me, xpeer[e]) for e in range(1, NX)]
    for target in targets:
        pl.semaphore_signal(barrier, inc=1, device_id=target, device_id_type=MESH)

    loads = []

    def load(src, dst):
        copy = pltpu.make_async_copy(src, dst, in_sem.at[len(loads)])
        copy.start()
        loads.append(copy)

    load(kv.at[0, 1], chunks.at[OWN, pl.ds(0, L)])
    load(kv.at[1, 1], chunks.at[OWN, pl.ds(L, L)])
    load(slot, slotv)
    load(order, orderv)
    load(start, startv)
    load(pick, pickv)
    load(freq, freqv)
    load(fkv.at[0], fkvv)
    load(kv.at[:, 0], kin)
    load(fq.at[0], fqv)
    load(dlen, dlenv)
    load(dq, dqv)
    load(dkv, dkvv)
    load(w, wv)

    def edge(d, i, way, n, src, dst):
        rows = pl.ds(*PIECES[i])
        sems = (rs_sem, rr_sem) if way == 0 else (ls_sem, lr_sem)
        return pltpu.make_async_remote_copy(
            src_ref=chunks.at[src, rows], dst_ref=chunks.at[dst, rows],
            send_sem=sems[0].at[d - 1, i], recv_sem=sems[1].at[d - 1, i],
            device_id=(zpeer[n, way], head), device_id_type=MESH,
        )

    def spot(d, way):
        return 2 * (d - 1) + way

    def arrived(d, i, way):
        edge(d, i, way, 1, spot(d, way), spot(d, way)).wait_recv()

    first = [[edge(1, i, way, 1, OWN, spot(1, way)) for way in (0, 1)] for i in range(NP)]
    for copy in loads[:2]:
        copy.wait()
    pl.semaphore_wait(barrier, len(targets))
    for copy in first[0]:
        copy.start()

    for copy in loads[2:8]:
        copy.wait()
    sub = iota((SLOTS, SLOTS), 0)
    lane = iota((SLOTS, SLOTS), 1)
    slot_row = slotv[...].astype(F32)
    start_row = startv[...].astype(F32)
    slot_col = jnp.sum(jnp.where(sub == lane, slot_row, 0.0), axis=1, keepdims=True)
    held = jnp.sum(jnp.where(orderv[...] == sub, slot_col, 0.0), axis=0, keepdims=True)
    lane_row = iota((1, SLOTS), 1)
    pick_t = pickv[...].astype(F32)
    fresh_place = pick_t + start_row
    freq_row = freqv[...]
    flip = jnp.where(iota((1, HD), 1) < HD // 2, -1.0, 1.0)

    own_place = jnp.sum(jnp.where(lane_row == me, fresh_place, 0.0), axis=1, keepdims=True)
    angle = own_place * freq_row
    fcos, fsin = jnp.cos(angle), jnp.sin(angle) * flip
    own_row = (me * 2).astype(F32)
    starts = [
        jnp.sum(jnp.where(held == own_row + float(i), start_row, 0.0), axis=1, keepdims=True)
        for i in range(2)
    ]
    cangle = jnp.concatenate([s * freq_row for s in starts], axis=0)
    ccos, csin = jnp.cos(cangle), jnp.sin(cangle) * flip

    pair = fkvv[...].astype(F32)
    fk = turn(pair[:, 0, :], fcos, fsin)
    chunks[OWN, 2 * L + 2 * L :, :] = jnp.concatenate([fk, pair[:, 1, :]], axis=0).astype(BF16)
    loads[8].wait()
    for i in range(2):
        turned = turn(kin[i].astype(F32), ccos[i : i + 1], csin[i : i + 1])
        chunks[OWN, 2 * L + L * i : 2 * L + L * (i + 1), :] = turned.astype(BF16)
    loads[9].wait()
    q_own = jnp.concatenate(
        [turn(fqv[:, HD * g : HD * (g + 1)].astype(F32), fcos, fsin) for g in range(G)], axis=0
    ).astype(BF16)
    queries[0:128, :] = q_own[0:128]
    queries[512:576, :] = q_own[128:192]

    for copy in first[1]:
        copy.start()

    qcopies = []
    for d in range(1, NY):
        at = NY - d
        for part, (src, dst, n) in enumerate(((0, 128 * at, 128), (512, 512 + 64 * at, 64))):
            copy = pltpu.make_async_remote_copy(
                src_ref=queries.at[pl.ds(src, n)], dst_ref=queries.at[pl.ds(dst, n)],
                send_sem=qs_sem.at[d - 1, part], recv_sem=qr_sem.at[d - 1, part],
                device_id=(ypeer[d], head), device_id_type=MESH,
            )
            copy.start()
            qcopies.append(copy)

    for copy in loads[10:13]:
        copy.wait()
    for g in range(G):
        queries[768 + ROWS * g : 768 + ROWS * (g + 1), :] = dqv[:, HD * g : HD * (g + 1)]

    tok = sub.astype(F32)
    hit = jnp.zeros((L, SLOTS), F32)
    for r in range(R):
        hit = jnp.where(pick_t[r : r + 1, :] == tok, 1.0, hit)
    table = jnp.where(hit > 0.0, BIG, start_row + tok)

    def fill(zs, carry):
        pool = zs * NY + y
        for i in range(2):
            row = (pool * 2 + i).astype(F32)
            here = jnp.min(jnp.where(held == row, table, BIG), axis=1, keepdims=True)
            places[zs, L * i : L * (i + 1), :] = jnp.broadcast_to(here, (L, HD))
        here = jnp.sum(jnp.where(lane_row == pool, fresh_place, 0.0), axis=1, keepdims=True)
        places[zs, 2 * L :, :] = jnp.broadcast_to(here, (R, HD))
        return carry

    lax.fori_loop(0, NZ, fill, 0)

    lam = iota((R, 1024), 1)
    tail = lam - 512
    q_in = jnp.where(lam < 512, lam & 127, 128 + (tail & 63))
    q_tok = q_in - R * ((q_in * 171) >> 12)
    spread = jnp.where(q_tok == iota((R, 1024), 0), 1.0, 0.0).astype(BF16)
    q_pick = tn(pick_t.astype(BF16), spread)
    start_col = jnp.sum(jnp.where(sub == lane, start_row, 0.0), axis=1, keepdims=True)
    lam1 = iota((1, 1024), 1)
    rel = jnp.where(lam1 < 512, lam1 >> 7, (lam1 - 512) >> 6)
    q_slot = z * NY + ((y + rel) & (NY - 1))
    slot_id = iota((SLOTS, 1024), 0)
    fresh_bound = jnp.sum(
        jnp.where(slot_id == q_slot, q_pick + start_col, 0.0), axis=0, keepdims=True
    )
    row_of = jnp.where((iota((ROWS, 1024), 1) & (ROWS - 1)) == iota((ROWS, 1024), 0), 1.0, 0.0)
    lens = jnp.dot(
        jnp.broadcast_to(dlenv[...].astype(F32), (8, ROWS)).astype(BF16), row_of.astype(BF16),
        preferred_element_type=F32,
    )[0:1]
    dec_bound = jnp.sum(
        jnp.where(slot_id.astype(F32) == lens, start_col - 1.0, 0.0), axis=0, keepdims=True
    )
    dec_bound = jnp.where(lens > SLOTS - 0.5, 0.5 * BIG, dec_bound)
    bounds[...] = jnp.where(lam1 < 768, fresh_bound, dec_bound)

    top[...] = jnp.full((1, 1024), FLOOR, F32)
    tot[...] = jnp.zeros((1, 1024), F32)
    acc[...] = jnp.zeros((HD, 1024), F32)
    own = dkvv[...].astype(F32)
    s = nt(own[:, 0, :].astype(BF16), queries[768:1024, :]) * C2
    mine = (iota((ROWS, 256), 1) & (ROWS - 1)) == iota((ROWS, 256), 0)
    s = jnp.where(mine & (y == 0), s, NEG)
    m = jnp.maximum(jnp.max(s, axis=0, keepdims=True), FLOOR)
    p = jnp.exp2(s - m)
    top[:, 768:1024] = m
    tot[:, 768:1024] = jnp.sum(p, axis=0, keepdims=True)
    acc[:, 768:1024] = tn(own[:, 1, :].astype(BF16), p.astype(BF16))

    for i in range(NP):
        for way in (0, 1):
            arrived(1, i, way)
            edge(2, i, way, 1, spot(1, way), spot(2, way)).start()
    for copy in qcopies:
        copy.wait_recv()

    def block(parts, b):
        cols = slice(QB * b, QB * (b + 1))
        fresh = [chunks[c, 256:304, :].astype(F32) for c, _ in parts]
        keys = jnp.concatenate(
            [chunks[c, 128:256, :] for c, _ in parts]
            + [jnp.concatenate([f[:R] for f in fresh], axis=0).astype(BF16)], axis=0)
        values = jnp.concatenate(
            [chunks[c, 0:128, :] for c, _ in parts]
            + [jnp.concatenate([f[R:] for f in fresh], axis=0).astype(BF16)], axis=0)
        at = [places[zs] for _, zs in parts]
        place = jnp.concatenate([a[:128] for a in at] + [a[128:] for a in at], axis=0)
        place = jnp.concatenate([place] * (QB // HD), axis=1)
        s = nt(keys, queries[cols, :]) * C2
        s = jnp.where(place <= bounds[:, cols], s, NEG)
        old = top[:, cols]
        new = jnp.maximum(old, jnp.max(s, axis=0, keepdims=True))
        p = jnp.exp2(s - new)
        fade = jnp.exp2(old - new)
        top[:, cols] = new
        tot[:, cols] = tot[:, cols] * fade + jnp.sum(p, axis=0, keepdims=True)
        acc[:, cols] = acc[:, cols] * fade + tn(values, p.astype(BF16))

    def ring_pair(d):
        return [(spot(d, 0), (z + NZ - d) % NZ), (spot(d, 1), (z + d) % NZ)]

    far = [edge(8, i, i, 2, spot(6, i), FAR) for i in range(NP)]

    for b in range(NQB):
        block([(OWN, z)], b)
    for b in (0, 1):
        block(ring_pair(1), b)
    for i in range(NP):
        for way in (0, 1):
            arrived(2, i, way)
            edge(4, i, way, 2, spot(2, way), spot(4, way)).start()
            edge(3, i, way, 1, spot(2, way), spot(3, way)).start()
    for b in (2, 3):
        block(ring_pair(1), b)
    for b in range(NQB):
        block(ring_pair(2), b)

    def stage(s, carry):
        d = 2 * s + 2
        for i in range(NP):
            for way in (0, 1):
                arrived(d, i, way)

                @pl.when(s == 1)
                def _():
                    edge(6, i, way, 2, spot(4, way), spot(6, way)).start()

                if i == way:
                    @pl.when(s == 2)
                    def _():
                        far[i].start()

                edge(d + 1, i, way, 1, spot(d, way), spot(d + 1, way)).start()
        for i in range(NP):
            for way in (0, 1):
                arrived(d - 1, i, way)
        for b in range(NQB):
            block(ring_pair(d - 1), b)
        for b in range(NQB):
            block(ring_pair(d), b)
        return carry

    lax.fori_loop(1, 3, stage, 0)
    for i in range(NP):
        for way in (0, 1):
            arrived(7, i, way)
    for copy in far:
        copy.wait_recv()

    def ycopy(src, dst, send, recv, d):
        return pltpu.make_async_remote_copy(
            src_ref=src, dst_ref=dst, send_sem=send, recv_sem=recv,
            device_id=(ypeer[d], head), device_id_type=MESH,
        )

    def pack(tile):
        cols = slice(HD * tile, HD * (tile + 1))
        part = acc[:, cols].astype(BF16)
        stat = jnp.concatenate([top[:, cols], tot[:, cols], jnp.zeros((6, HD), F32)], axis=0)
        if tile < 6:
            fsend[tile] = part
            fstat[tile] = stat
        else:
            dsend[tile - 6] = part
            dstat[tile - 6] = stat

    last = ring_pair(7) + [(FAR, (z + NZ // 2) % NZ)]
    block(last, 3)
    pack(6)
    pack(7)
    dcopies, fcopies = [], []
    for d in range(1, NY):
        dcopies.append(ycopy(dstat, dsrecv.at[d - 1], ds_sem.at[d - 1, 1], dr_sem.at[d - 1, 1], d))
        dcopies.append(ycopy(dsend, drecv.at[d - 1], ds_sem.at[d - 1, 0], dr_sem.at[d - 1, 0], d))
    for copy in dcopies:
        copy.start()
    for b in range(3):
        block(last, b)
        pack(2 * b)
        pack(2 * b + 1)
    for d in range(1, NY):
        for part, tile in enumerate((d, 4 + d // 2)):
            fcopies.append(ycopy(fstat.at[tile], fsrecv.at[d - 1, part],
                                 fs_sem.at[d - 1, 2 + part], fr_sem.at[d - 1, 2 + part], d))
            fcopies.append(ycopy(fsend.at[tile], frecv.at[d - 1, part],
                                 fs_sem.at[d - 1, part], fr_sem.at[d - 1, part], d))
    for copy in fcopies:
        copy.start()

    def blend(parts):
        peak = functools.reduce(jnp.maximum, [m for m, _, _ in parts])
        total, mixed = 0.0, 0.0
        for m, l, a in parts:
            scale = jnp.exp2(m - peak)
            total = total + l * scale
            mixed = mixed + a * scale
        return mixed / total

    for copy in dcopies:
        copy.wait_recv()
    halves = []
    for tile in range(2):
        cols = slice(768 + HD * tile, 768 + HD * (tile + 1))
        parts = [(top[:, cols], tot[:, cols], acc[:, cols])]
        for d in range(NY - 1):
            stat = dsrecv[d, tile]
            parts.append((stat[0:1], stat[1:2], drecv[d, tile].astype(F32)))
        halves.append(blend(parts).T)
    whole = jnp.concatenate(halves, axis=0)
    attended = jnp.concatenate(
        [whole[ROWS * g : ROWS * (g + 1)] for g in range(G)], axis=1
    ).astype(BF16)
    loads[13].wait()
    halfs[core] = jnp.dot(attended, wv[...], preferred_element_type=F32)
    swap = pltpu.make_async_remote_copy(
        src_ref=halfs.at[core], dst_ref=halfs.at[core], send_sem=xs_sem.at[0], recv_sem=xr_sem.at[0],
        device_id=(me, mate), device_id_type=MESH,
    )
    swap.start()
    swap.wait_recv()
    terms[column] = halfs[0] + halfs[1]
    xcopies = []
    for e in range(1, NX):
        copy = pltpu.make_async_remote_copy(
            src_ref=terms.at[column], dst_ref=terms.at[column],
            send_sem=xs_sem.at[e], recv_sem=xr_sem.at[e],
            device_id=(me, xpeer[e]), device_id_type=MESH,
        )
        copy.start()
        xcopies.append(copy)

    for copy in fcopies:
        copy.wait_recv()
    outs = []
    for part in range(2):
        cols = slice(512 * part, 512 * part + HD)
        parts = [(top[:, cols], tot[:, cols], acc[:, cols])]
        for d in range(1, NY):
            stat = fsrecv[d - 1, part]
            a = frecv[d - 1, part].astype(F32)
            if part == 1 and d % 2 == 1:
                stat = pltpu.roll(stat, HD // 2, 1)
                a = pltpu.roll(a, HD // 2, 1)
            parts.append((stat[0:1], stat[1:2], a))
        outs.append(blend(parts).T)
    rows = jnp.concatenate([outs[0], outs[1][:64]], axis=0)
    fresh_out[0] = jnp.concatenate(
        [rows[R * g : R * (g + 1)] for g in range(G)], axis=1
    ).astype(BF16)

    for e in range(1, NX):
        source = (column + NX - e) % NX
        pltpu.make_async_remote_copy(
            src_ref=terms.at[source], dst_ref=terms.at[source],
            send_sem=xs_sem.at[e], recv_sem=xr_sem.at[e],
            device_id=(me, xpeer[e]), device_id_type=MESH,
        ).wait_recv()
    total = terms[0]
    for c in range(1, NX):
        total = total + terms[c]
    dec_out[...] = total.astype(BF16)

    for copy in first[0] + first[1] + far + qcopies + dcopies + fcopies + [swap] + xcopies:
        copy.wait_send()
    for d in range(2, 8):
        for i in range(NP):
            for way in (0, 1):
                edge(d, i, way, 1, spot(d, way), spot(d, way)).wait_send()


def shards(
    kv_store, fresh_q, fresh_kv, dec_q, dec_kv, out_weight,
    span_slot, span_order, span_start, pick, dec_len,
):
    half = HD // 2
    freq = np.power(BASE, -np.arange(half, dtype=np.float64) / half).astype(np.float32)
    freq = jnp.asarray(np.concatenate([freq, freq])[None, :])
    dma = pltpu.SemaphoreType.DMA
    vmem = pltpu.VMEM
    return pl.pallas_call(
        kernel,
        out_shape=(
            vmem((1, R, G * HD), BF16),
            vmem((ROWS, HD), BF16),
        ),
        in_specs=[pl.BlockSpec(memory_space=pl.ANY)] * 12,
        out_specs=(pl.BlockSpec(memory_space=vmem), pl.BlockSpec(memory_space=vmem)),
        scratch_shapes=[
            vmem((2, L, HD), BF16),
            vmem((R, G * HD), BF16),
            vmem((R, 2, HD), BF16),
            vmem((ROWS, G * HD), BF16),
            vmem((ROWS, 2, HD), BF16),
            vmem((G * HD, HD), BF16),
            vmem((1, SLOTS), jnp.int32),
            vmem((1, SLOTS), jnp.int32),
            vmem((1, SLOTS), jnp.int32),
            vmem((R, SLOTS), jnp.int32),
            vmem((1, ROWS), jnp.int32),
            vmem((1, HD), F32),
            vmem((NZ, CH, HD), BF16),
            vmem((1024, HD), BF16),
            vmem((NZ, 2 * L + R, HD), F32),
            vmem((1, 1024), F32),
            vmem((1, 1024), F32),
            vmem((1, 1024), F32),
            vmem((HD, 1024), F32),
            vmem((2, HD, HD), BF16),
            vmem((2, 8, HD), F32),
            vmem((6, HD, HD), BF16),
            vmem((6, 8, HD), F32),
            vmem((NY - 1, 2, HD, HD), BF16),
            vmem((NY - 1, 2, 8, HD), F32),
            vmem((NY - 1, 2, HD, HD), BF16),
            vmem((NY - 1, 2, 8, HD), F32),
            vmem((2, ROWS, HD), F32),
            vmem((NX, ROWS, HD), F32),
            dma((14,)),
            dma((8, NP)), dma((8, NP)), dma((8, NP)), dma((8, NP)),
            dma((NY - 1, 2)), dma((NY - 1, 2)),
            dma((NY - 1, 2)), dma((NY - 1, 2)),
            dma((NY - 1, 4)), dma((NY - 1, 4)),
            dma((NX,)), dma((NX,)),
        ],
        compiler_params=pltpu.CompilerParams(collective_id=0, has_side_effects=True),
        name="layer",
    )(
        kv_store, fresh_q, fresh_kv, dec_q, dec_kv, out_weight,
        span_slot[None, :], span_order[None, :], span_start[None, :], pick.T, dec_len[None, :], freq,
    )


def solution(mesh):
    return jax.shard_map(
        shards,
        mesh=mesh,
        in_specs=(
            P("pool", None, None, "head"),
            P("pool", None, "head"),
            P("pool", None, None, "head"),
            P(None, "head"),
            P(None, None, "head"),
            P("head", "pool"),
            P(), P(), P(), P(), P(),
        ),
        out_specs=(P("pool", None, "head"), P(None, "pool")),
        check_vma=False,
    )
```

time: 1470 us -> 50.1 us (0.03)
  the two profiles are of different devices: /device:TPU:504 before, /device:TPU:1 now
where the time goes in v1:
time: 50.1 us; the launch traced here: 49.9 us
  Pallas kernels  48.1 us (96%)
  local copies, waits for them, and re-layouts  1.22 us (2%)
  between operations  0.64 us (1%)
    pallas_call x1, Pallas kernels, shards(): pl.pallas_call(kernel, out_shape=(vmem((1, R, G * HD), BF16), vmem((ROWS,...  48.1 us
    unnamed x2, local copies, waits for them, and re-layouts  1.22 us

profile of v1, /device:TPU:1, one launch (start us, length us, event | category | flops | bytes accessed | tf_op | source)
XLA Modules:
  0.0 49.9 jit_solution(4819269464134888602)
XLA Ops:
  0.6 48.1 %layer.1 = (bf16[1,24,1024]{2,1,0:T(8,128)(2,1)S(1)}, bf16[32,128]{1,0:T(8,128)(2,1)S(1)}) custom-call(bf16[2,2,64,128]{3,2,1,0:T(8,128)(2,1)} %kv.1, bf16[1,24,1024]{2,1,0:T(8,128)(2,1)} %fq.1, bf16[1,24,2,128]{3,2,1,0:T(2,128)(2,1)} %fkv.1, bf16[32,1024]{1,0:T(8,128)(2,1)} %dq.1, bf16[32,2,128]{2,1,0:T(2,128)(2,1)} %dkv.1, bf16[1024,128]{1,0:T(8,128)(2,1)} %w.1, ...), custom_call_target="tpu_custom_call" | custom-call | tf_op jit(solution)/shard_map/layer/pallas_call | solution.py:445
  48.7 0.6 %copy.16 = bf16[1,24,1024]{2,1,0:T(8,128)(2,1)} copy(bf16[1,24,1024]{2,1,0:T(8,128)(2,1)S(1)} %get-tuple-element.2) | data formatting | bytes 98304
  49.3 0.6 %copy.17 = bf16[32,128]{1,0:T(8,128)(2,1)} copy(bf16[32,128]{1,0:T(8,128)(2,1)S(1)} %get-tuple-element.3) | data formatting | bytes 16384

commit v2 on v1

--- a/solution.py
+++ b/solution.py
@@ -50,7 +50,7 @@
     fresh_out, dec_out,
     kin, fqv, fkvv, dqv, dkvv, wv, slotv, orderv, startv, pickv, dlenv, freqv,
     chunks, queries, places, bounds, top, tot, acc,
-    dsend, dstat, fsend, fstat, drecv, dsrecv, frecv, fsrecv, halfs, terms,
+    send, drecv, frecv, halfs, terms,
     in_sem, rs_sem, rr_sem, ls_sem, lr_sem, qs_sem, qr_sem,
     ds_sem, dr_sem, fs_sem, fr_sem, xs_sem, xr_sem,
 ):
@@ -61,15 +61,12 @@
     ring = NZ * NY
     zpeer = {(n, way): (me + ring + (n if way == 0 else -n) * NY) % ring for n in (1, 2) for way in (0, 1)}
     ypeer = [z * NY + (y + d) % NY for d in range(NY)]
-    core = head % 2
-    column = head // 2
-    mate = head + 1 - 2 * core
-    xpeer = [(head + 2 * e) % NH for e in range(NX)]
+    hpeer = [(head + e) % NH for e in range(NH)]
 
     barrier = pltpu.get_barrier_semaphore()
     targets = [(zpeer[n, way], head) for n in (1, 2) for way in (0, 1)]
     targets += [(ypeer[d], head) for d in range(1, NY)]
-    targets += [(me, mate)] + [(me, xpeer[e]) for e in range(1, NX)]
+    targets += [(me, hpeer[e]) for e in range(1, NH)]
     for target in targets:
         pl.semaphore_signal(barrier, inc=1, device_id=target, device_id_type=MESH)
 
@@ -111,12 +108,6 @@
         edge(d, i, way, 1, spot(d, way), spot(d, way)).wait_recv()
 
     first = [[edge(1, i, way, 1, OWN, spot(1, way)) for way in (0, 1)] for i in range(NP)]
-    for copy in loads[:2]:
-        copy.wait()
-    pl.semaphore_wait(barrier, len(targets))
-    for copy in first[0]:
-        copy.start()
-
     for copy in loads[2:8]:
         copy.wait()
     sub = iota((SLOTS, SLOTS), 0)
@@ -149,15 +140,17 @@
     for i in range(2):
         turned = turn(kin[i].astype(F32), ccos[i : i + 1], csin[i : i + 1])
         chunks[OWN, 2 * L + L * i : 2 * L + L * (i + 1), :] = turned.astype(BF16)
+    for copy in loads[:2]:
+        copy.wait()
+    pl.semaphore_wait(barrier, len(targets))
+    for copy in first[0] + first[1]:
+        copy.start()
     loads[9].wait()
     q_own = jnp.concatenate(
         [turn(fqv[:, HD * g : HD * (g + 1)].astype(F32), fcos, fsin) for g in range(G)], axis=0
     ).astype(BF16)
     queries[0:128, :] = q_own[0:128]
     queries[512:576, :] = q_own[128:192]
-
-    for copy in first[1]:
-        copy.start()
 
     qcopies = []
     for d in range(1, NY):
@@ -318,16 +311,25 @@
             device_id=(ypeer[d], head), device_id_type=MESH,
         )
 
+    def split(row):
+        high = row.astype(BF16)
+        rest = row - high.astype(F32)
+        mid = rest.astype(BF16)
+        return [high.astype(F32), mid.astype(F32), rest - mid.astype(F32)]
+
     def pack(tile):
         cols = slice(HD * tile, HD * (tile + 1))
-        part = acc[:, cols].astype(BF16)
-        stat = jnp.concatenate([top[:, cols], tot[:, cols], jnp.zeros((6, HD), F32)], axis=0)
-        if tile < 6:
-            fsend[tile] = part
-            fstat[tile] = stat
-        else:
-            dsend[tile - 6] = part
-            dstat[tile - 6] = stat
+        stat = split(top[:, cols]) + split(tot[:, cols]) + [jnp.zeros((10, HD), F32)]
+        send[tile, :HD, :] = acc[:, cols].astype(BF16)
+        send[tile, HD:, :] = jnp.concatenate(stat, axis=0).astype(BF16)
+
+    def unpack(block):
+        stat = block[HD:].astype(F32)
+        return (
+            stat[0:1] + stat[1:2] + stat[2:3],
+            stat[3:4] + stat[4:5] + stat[5:6],
+            block[:HD].astype(F32),
+        )
 
     last = ring_pair(7) + [(FAR, (z + NZ // 2) % NZ)]
     block(last, 3)
@@ -335,8 +337,7 @@
     pack(7)
     dcopies, fcopies = [], []
     for d in range(1, NY):
-        dcopies.append(ycopy(dstat, dsrecv.at[d - 1], ds_sem.at[d - 1, 1], dr_sem.at[d - 1, 1], d))
-        dcopies.append(ycopy(dsend, drecv.at[d - 1], ds_sem.at[d - 1, 0], dr_sem.at[d - 1, 0], d))
+        dcopies.append(ycopy(send.at[pl.ds(6, 2)], drecv.at[d - 1], ds_sem.at[d - 1], dr_sem.at[d - 1], d))
     for copy in dcopies:
         copy.start()
     for b in range(3):
@@ -345,9 +346,7 @@
         pack(2 * b + 1)
     for d in range(1, NY):
         for part, tile in enumerate((d, 4 + d // 2)):
-            fcopies.append(ycopy(fstat.at[tile], fsrecv.at[d - 1, part],
-                                 fs_sem.at[d - 1, 2 + part], fr_sem.at[d - 1, 2 + part], d))
-            fcopies.append(ycopy(fsend.at[tile], frecv.at[d - 1, part],
+            fcopies.append(ycopy(send.at[tile], frecv.at[d - 1, part],
                                  fs_sem.at[d - 1, part], fr_sem.at[d - 1, part], d))
     for copy in fcopies:
         copy.start()
@@ -368,28 +367,20 @@
         cols = slice(768 + HD * tile, 768 + HD * (tile + 1))
         parts = [(top[:, cols], tot[:, cols], acc[:, cols])]
         for d in range(NY - 1):
-            stat = dsrecv[d, tile]
-            parts.append((stat[0:1], stat[1:2], drecv[d, tile].astype(F32)))
+            parts.append(unpack(drecv[d, tile]))
         halves.append(blend(parts).T)
     whole = jnp.concatenate(halves, axis=0)
     attended = jnp.concatenate(
         [whole[ROWS * g : ROWS * (g + 1)] for g in range(G)], axis=1
     ).astype(BF16)
     loads[13].wait()
-    halfs[core] = jnp.dot(attended, wv[...], preferred_element_type=F32)
-    swap = pltpu.make_async_remote_copy(
-        src_ref=halfs.at[core], dst_ref=halfs.at[core], send_sem=xs_sem.at[0], recv_sem=xr_sem.at[0],
-        device_id=(me, mate), device_id_type=MESH,
-    )
-    swap.start()
-    swap.wait_recv()
-    terms[column] = halfs[0] + halfs[1]
+    terms[head] = jnp.dot(attended, wv[...], preferred_element_type=F32)
     xcopies = []
-    for e in range(1, NX):
+    for e in (4, 3, 5, 2, 6, 7, 1):
         copy = pltpu.make_async_remote_copy(
-            src_ref=terms.at[column], dst_ref=terms.at[column],
+            src_ref=terms.at[head], dst_ref=terms.at[head],
             send_sem=xs_sem.at[e], recv_sem=xr_sem.at[e],
-            device_id=(me, xpeer[e]), device_id_type=MESH,
+            device_id=(me, hpeer[e]), device_id_type=MESH,
         )
         copy.start()
         xcopies.append(copy)
@@ -401,31 +392,29 @@
         cols = slice(512 * part, 512 * part + HD)
         parts = [(top[:, cols], tot[:, cols], acc[:, cols])]
         for d in range(1, NY):
-            stat = fsrecv[d - 1, part]
-            a = frecv[d - 1, part].astype(F32)
+            m, l, a = unpack(frecv[d - 1, part])
             if part == 1 and d % 2 == 1:
-                stat = pltpu.roll(stat, HD // 2, 1)
-                a = pltpu.roll(a, HD // 2, 1)
-            parts.append((stat[0:1], stat[1:2], a))
+                m, l, a = (pltpu.roll(v, HD // 2, 1) for v in (m, l, a))
+            parts.append((m, l, a))
         outs.append(blend(parts).T)
     rows = jnp.concatenate([outs[0], outs[1][:64]], axis=0)
     fresh_out[0] = jnp.concatenate(
         [rows[R * g : R * (g + 1)] for g in range(G)], axis=1
     ).astype(BF16)
 
-    for e in range(1, NX):
-        source = (column + NX - e) % NX
+    for e in range(1, NH):
+        source = (head + NH - e) % NH
         pltpu.make_async_remote_copy(
             src_ref=terms.at[source], dst_ref=terms.at[source],
             send_sem=xs_sem.at[e], recv_sem=xr_sem.at[e],
-            device_id=(me, xpeer[e]), device_id_type=MESH,
+            device_id=(me, hpeer[e]), device_id_type=MESH,
         ).wait_recv()
     total = terms[0]
-    for c in range(1, NX):
-        total = total + terms[c]
+    for h in range(1, NH):
+        total = total + terms[h]
     dec_out[...] = total.astype(BF16)
 
-    for copy in first[0] + first[1] + far + qcopies + dcopies + fcopies + [swap] + xcopies:
+    for copy in first[0] + first[1] + far + qcopies + dcopies + fcopies + xcopies:
         copy.wait_send()
     for d in range(2, 8):
         for i in range(NP):
@@ -470,22 +459,17 @@
             vmem((1, 1024), F32),
             vmem((1, 1024), F32),
             vmem((HD, 1024), F32),
-            vmem((2, HD, HD), BF16),
-            vmem((2, 8, HD), F32),
-            vmem((6, HD, HD), BF16),
-            vmem((6, 8, HD), F32),
-            vmem((NY - 1, 2, HD, HD), BF16),
-            vmem((NY - 1, 2, 8, HD), F32),
-            vmem((NY - 1, 2, HD, HD), BF16),
-            vmem((NY - 1, 2, 8, HD), F32),
+            vmem((8, HD + 16, HD), BF16),
+            vmem((NY - 1, 2, HD + 16, HD), BF16),
+            vmem((NY - 1, 2, HD + 16, HD), BF16),
             vmem((2, ROWS, HD), F32),
-            vmem((NX, ROWS, HD), F32),
+            vmem((NH, ROWS, HD), F32),
             dma((14,)),
             dma((8, NP)), dma((8, NP)), dma((8, NP)), dma((8, NP)),
             dma((NY - 1, 2)), dma((NY - 1, 2)),
+            dma((NY - 1,)), dma((NY - 1,)),
             dma((NY - 1, 2)), dma((NY - 1, 2)),
-            dma((NY - 1, 4)), dma((NY - 1, 4)),
-            dma((NX,)), dma((NX,)),
+            dma((NH,)), dma((NH,)),
         ],
         compiler_params=pltpu.CompilerParams(collective_id=0, has_side_effects=True),
         name="layer",

time: 50.1 us -> 49.2 us (0.982)
  Pallas kernels: 48.1 us -> 47.3 us
    pallas_call x1, Pallas kernels: 48.1 us -> 47.3 us  [shards(): pl.pallas_call(kernel, out_shape=(vmem((1, R, G * HD), BF16), vmem((ROWS,...]
where the time goes in v2:
time: 49.2 us; the launch traced here: 49.1 us
  Pallas kernels  47.3 us (96%)
  local copies, waits for them, and re-layouts  1.22 us (2%)
  between operations  0.64 us (1%)
    pallas_call x1, Pallas kernels, shards(): pl.pallas_call(kernel, out_shape=(vmem((1, R, G * HD), BF16), vmem((ROWS,...  47.3 us
    unnamed x2, local copies, waits for them, and re-layouts  1.22 us

profile of v2, /device:TPU:1, one launch (start us, length us, event | category | flops | bytes accessed | tf_op | source)
XLA Modules:
  0.0 49.1 jit_solution(3711952482231216732)
XLA Ops:
  0.6 47.3 %layer.1 = (bf16[1,24,1024]{2,1,0:T(8,128)(2,1)S(1)}, bf16[32,128]{1,0:T(8,128)(2,1)S(1)}) custom-call(bf16[2,2,64,128]{3,2,1,0:T(8,128)(2,1)} %kv.1, bf16[1,24,1024]{2,1,0:T(8,128)(2,1)} %fq.1, bf16[1,24,2,128]{3,2,1,0:T(2,128)(2,1)} %fkv.1, bf16[32,1024]{1,0:T(8,128)(2,1)} %dq.1, bf16[32,2,128]{2,1,0:T(2,128)(2,1)} %dkv.1, bf16[1024,128]{1,0:T(8,128)(2,1)} %w.1, ...), custom_call_target="tpu_custom_call" | custom-call | tf_op jit(solution)/shard_map/layer/pallas_call | solution.py:434
  47.9 0.6 %copy.16 = bf16[1,24,1024]{2,1,0:T(8,128)(2,1)} copy(bf16[1,24,1024]{2,1,0:T(8,128)(2,1)S(1)} %get-tuple-element.2) | data formatting | bytes 98304
  48.5 0.6 %copy.17 = bf16[32,128]{1,0:T(8,128)(2,1)} copy(bf16[32,128]{1,0:T(8,128)(2,1)S(1)} %get-tuple-element.3) | data formatting | bytes 16384

commit v3 on v2

--- a/solution.py
+++ b/solution.py
@@ -19,7 +19,7 @@
 BIG = 1e9
 C2 = HD**-0.5 * math.log2(math.e)
 CH = 304
-PIECES = ((0, 128), (128, 176))
+PIECES = ((0, 144), (144, 160))
 NP = len(PIECES)
 OWN, FAR = 14, 15
 QB = 256
@@ -107,7 +107,9 @@
     def arrived(d, i, way):
         edge(d, i, way, 1, spot(d, way), spot(d, way)).wait_recv()
 
-    first = [[edge(1, i, way, 1, OWN, spot(1, way)) for way in (0, 1)] for i in range(NP)]
+    first = [
+        [edge(n, i, way, n, OWN, spot(n, way)) for way in (0, 1) for i in range(NP)] for n in (2, 1)
+    ]
     for copy in loads[2:8]:
         copy.wait()
     sub = iota((SLOTS, SLOTS), 0)
@@ -227,8 +229,11 @@
 
     for i in range(NP):
         for way in (0, 1):
-            arrived(1, i, way)
-            edge(2, i, way, 1, spot(1, way), spot(2, way)).start()
+            arrived(2, i, way)
+            edge(4, i, way, 2, spot(2, way), spot(4, way)).start()
+    for i in range(NP):
+        for way in (0, 1):
+            edge(3, i, way, 1, spot(2, way), spot(3, way)).start()
     for copy in qcopies:
         copy.wait_recv()
 
@@ -261,13 +266,11 @@
 
     for b in range(NQB):
         block([(OWN, z)], b)
+    for i in range(NP):
+        for way in (0, 1):
+            arrived(1, i, way)
     for b in (0, 1):
         block(ring_pair(1), b)
-    for i in range(NP):
-        for way in (0, 1):
-            arrived(2, i, way)
-            edge(4, i, way, 2, spot(2, way), spot(4, way)).start()
-            edge(3, i, way, 1, spot(2, way), spot(3, way)).start()
     for b in (2, 3):
         block(ring_pair(1), b)
     for b in range(NQB):
@@ -288,6 +291,8 @@
                     def _():
                         far[i].start()
 
+        for i in range(NP):
+            for way in (0, 1):
                 edge(d + 1, i, way, 1, spot(d, way), spot(d + 1, way)).start()
         for i in range(NP):
             for way in (0, 1):
@@ -336,7 +341,7 @@
     pack(6)
     pack(7)
     dcopies, fcopies = [], []
-    for d in range(1, NY):
+    for d in (2, 1, 3):
         dcopies.append(ycopy(send.at[pl.ds(6, 2)], drecv.at[d - 1], ds_sem.at[d - 1], dr_sem.at[d - 1], d))
     for copy in dcopies:
         copy.start()
@@ -416,7 +421,7 @@
 
     for copy in first[0] + first[1] + far + qcopies + dcopies + fcopies + xcopies:
         copy.wait_send()
-    for d in range(2, 8):
+    for d in range(3, 8):
         for i in range(NP):
             for way in (0, 1):
                 edge(d, i, way, 1, spot(d, way), spot(d, way)).wait_send()

time: 49.2 us -> 48.1 us (0.978)
  Pallas kernels: 47.3 us -> 46.1 us
    pallas_call x1, Pallas kernels: 47.3 us -> 46.1 us  [shards(): pl.pallas_call(kernel, out_shape=(vmem((1, R, G * HD), BF16), vmem((ROWS,...]
where the time goes in v3:
time: 48.1 us; the launch traced here: 48 us
  Pallas kernels  46.1 us (96%)
  local copies, waits for them, and re-layouts  1.22 us (3%)
  between operations  0.64 us (1%)
    pallas_call x1, Pallas kernels, shards(): pl.pallas_call(kernel, out_shape=(vmem((1, R, G * HD), BF16), vmem((ROWS,...  46.1 us
    unnamed x2, local copies, waits for them, and re-layouts  1.22 us

profile of v3, /device:TPU:1, one launch (start us, length us, event | category | flops | bytes accessed | tf_op | source)
XLA Modules:
  0.0 48.0 jit_solution(17133712124291903052)
XLA Ops:
  0.6 46.1 %layer.1 = (bf16[1,24,1024]{2,1,0:T(8,128)(2,1)S(1)}, bf16[32,128]{1,0:T(8,128)(2,1)S(1)}) custom-call(bf16[2,2,64,128]{3,2,1,0:T(8,128)(2,1)} %kv.1, bf16[1,24,1024]{2,1,0:T(8,128)(2,1)} %fq.1, bf16[1,24,2,128]{3,2,1,0:T(2,128)(2,1)} %fkv.1, bf16[32,1024]{1,0:T(8,128)(2,1)} %dq.1, bf16[32,2,128]{2,1,0:T(2,128)(2,1)} %dkv.1, bf16[1024,128]{1,0:T(8,128)(2,1)} %w.1, ...), custom_call_target="tpu_custom_call" | custom-call | tf_op jit(solution)/shard_map/layer/pallas_call | solution.py:439
  46.8 0.6 %copy.16 = bf16[1,24,1024]{2,1,0:T(8,128)(2,1)} copy(bf16[1,24,1024]{2,1,0:T(8,128)(2,1)S(1)} %get-tuple-element.2) | data formatting | bytes 98304
  47.4 0.6 %copy.17 = bf16[32,128]{1,0:T(8,128)(2,1)} copy(bf16[32,128]{1,0:T(8,128)(2,1)S(1)} %get-tuple-element.3) | data formatting | bytes 16384

commit v4 on v3

--- a/solution.py
+++ b/solution.py
@@ -407,6 +407,13 @@
         [rows[R * g : R * (g + 1)] for g in range(G)], axis=1
     ).astype(BF16)
 
+    for copy in first[0] + first[1] + far + qcopies + dcopies + fcopies:
+        copy.wait_send()
+    for d in range(3, 8):
+        for i in range(NP):
+            for way in (0, 1):
+                edge(d, i, way, 1, spot(d, way), spot(d, way)).wait_send()
+
     for e in range(1, NH):
         source = (head + NH - e) % NH
         pltpu.make_async_remote_copy(
@@ -419,12 +426,8 @@
         total = total + terms[h]
     dec_out[...] = total.astype(BF16)
 
-    for copy in first[0] + first[1] + far + qcopies + dcopies + fcopies + xcopies:
+    for copy in xcopies:
         copy.wait_send()
-    for d in range(3, 8):
-        for i in range(NP):
-            for way in (0, 1):
-                edge(d, i, way, 1, spot(d, way), spot(d, way)).wait_send()
 
 
 def shards(

time: 48.1 us -> 48 us (level)
  no operation moved by 1% of the time
where the time goes in v4:
time: 48 us; the launch traced here: 47.9 us
  Pallas kernels  46 us (96%)
  local copies, waits for them, and re-layouts  1.22 us (3%)
  between operations  0.64 us (1%)
    pallas_call x1, Pallas kernels, shards(): pl.pallas_call(kernel, out_shape=(vmem((1, R, G * HD), BF16), vmem((ROWS,...  46 us
    unnamed x2, local copies, waits for them, and re-layouts  1.22 us

profile of v4, /device:TPU:1, one launch (start us, length us, event | category | flops | bytes accessed | tf_op | source)
XLA Modules:
  0.0 47.9 jit_solution(2369798244183064382)
XLA Ops:
  0.6 46.0 %layer.1 = (bf16[1,24,1024]{2,1,0:T(8,128)(2,1)S(1)}, bf16[32,128]{1,0:T(8,128)(2,1)S(1)}) custom-call(bf16[2,2,64,128]{3,2,1,0:T(8,128)(2,1)} %kv.1, bf16[1,24,1024]{2,1,0:T(8,128)(2,1)} %fq.1, bf16[1,24,2,128]{3,2,1,0:T(2,128)(2,1)} %fkv.1, bf16[32,1024]{1,0:T(8,128)(2,1)} %dq.1, bf16[32,2,128]{2,1,0:T(2,128)(2,1)} %dkv.1, bf16[1024,128]{1,0:T(8,128)(2,1)} %w.1, ...), custom_call_target="tpu_custom_call" | custom-call | tf_op jit(solution)/shard_map/layer/pallas_call | solution.py:442
  46.7 0.6 %copy.16 = bf16[1,24,1024]{2,1,0:T(8,128)(2,1)} copy(bf16[1,24,1024]{2,1,0:T(8,128)(2,1)S(1)} %get-tuple-element.2) | data formatting | bytes 98304
  47.3 0.6 %copy.17 = bf16[32,128]{1,0:T(8,128)(2,1)} copy(bf16[32,128]{1,0:T(8,128)(2,1)S(1)} %get-tuple-element.3) | data formatting | bytes 16384
